TPU v7x, 128 devices: a whole 4x4x4 slice. The times are simulated.
128 devices in a mesh: col: 8 (over x, z_lo), row: 16 (over y, z_hi, core).
Axes of the slice: x: 4, y: 4, z: 4 (z_hi: 2, z_lo: 2; z = z_hi * 2 + z_lo), core: 2. Of those that a mesh axis runs over, the one named last changes fastest.
Arguments:
- covariance: float32 [12288, 12288], P('row', 'col'), may hold values from -2 to 2, as said below
- wfs_map: int32 [12288], P('row'), may hold values from 0 to 5
- noise_var: float32 [6], replicated, may hold values from 0.5 to 2
- targets: float32 [12288, 2048], P('row', 'col'), may hold values from -0.6 to 0.6
- target_pos: float32 [2, 2048], replicated, may hold values from -1 to 1
- layer_strength: float32 [35], replicated, may hold values from 0.005 to 0.05
- layer_scale: float32 [35], replicated, may hold values from 0.2 to 2
- tile_layer: int32 [16], replicated, may hold values from 0 to 34
Outputs:
- updated: float32 [12288, 12288], P('row', 'col')
- panel_factor: float32 [12288, 256], P('row')
- reconstructor: float32 [12288, 2048], P('row', 'col')
- error_cov: float32 [2048, 2048], P('row', 'col')
Inputs may be any that keep to these rules, and one draw needn't show every extreme that they name: `covariance`: symmetric and positive semidefinite; its diagonal lies between 0.5 and 2.
All inputs are finite; a program needn't handle non-finite values.
Results may differ from a plain program's by a relative error of at most 0.0003.
Values sent between devices are 32-bit elements; how exact they have to be, the bound alone decides.
No kernel may reach another device: no remote copies, remote signals or barrier semaphores. Data moves between devices by JAX's collectives and lax.ppermute only.
A program may use at most 64 MiB of HBM per device.

v0:
```python
import jax
import jax.numpy as jnp
from jax import lax
from jax.sharding import PartitionSpec as P

PB = 256
TILE = 128
precise = lax.Precision.HIGHEST


def broadcast(shard, axis, root):
    mine = lax.axis_index(axis) == root
    return lax.psum(jnp.where(mine, shard, jnp.zeros_like(shard)), axis)


def lookup(values, indices, entries):
    one_hot = (indices[:, None] == jnp.arange(entries, dtype=jnp.int32)[None, :]).astype(
        jnp.float32
    )
    return jnp.dot(one_hot, values, precision=precise)


def target_covariance(pos_rows, pos_cols, layer_rows, layer_cols, layer_strength, layer_scale):
    distance = (pos_rows[0][:, None] - pos_cols[0][None, :]) ** 2 + (
        pos_rows[1][:, None] - pos_cols[1][None, :]
    ) ** 2
    lowest = jnp.minimum(layer_rows[:, None], layer_cols[None, :])
    levels = jnp.arange(layer_strength.shape[0], dtype=jnp.int32)
    weights = layer_strength[:, None, None] / (
        1.0 + distance[None] / (layer_scale * layer_scale)[:, None, None]
    )
    return jnp.sum(jnp.where(levels[:, None, None] <= lowest[None], weights, 0.0), axis=0)


def local(
    covariance, wfs_map, noise_var, targets, target_pos, layer_strength, layer_scale, tile_layer
):
    row_count, col_count = covariance.shape
    target_width = targets.shape[1]
    row_index = lax.axis_index("row")
    col_index = lax.axis_index("col")
    row_ids = row_index * row_count + jnp.arange(row_count, dtype=jnp.int32)
    col_ids = col_index * col_count + jnp.arange(col_count, dtype=jnp.int32)
    noise_rows = lookup(noise_var, wfs_map, noise_var.shape[0])
    on_diagonal = row_ids[:, None] == col_ids[None, :]
    matrix = covariance + jnp.where(on_diagonal, noise_rows[:, None], 0.0)
    diag_block = broadcast(matrix[:PB, :PB], ("col", "row"), 0)
    factor = jnp.linalg.cholesky(diag_block)
    solved = jax.scipy.linalg.solve_triangular(factor, matrix[:, :PB].T, lower=True).T
    top_rows = jnp.concatenate([factor, jnp.zeros((row_count - PB, PB), jnp.float32)], axis=0)
    own_rows = jnp.where(row_ids[:, None] < PB, top_rows, solved)
    panel_rows = broadcast(own_rows, "col", 0)
    head_rows = jax.scipy.linalg.solve_triangular(factor, targets[:PB], lower=True)
    upper_rows = jax.scipy.linalg.solve_triangular(factor, matrix[:PB, :], lower=True)
    lead_cols = jnp.concatenate([factor.T, jnp.zeros((PB, col_count - PB), jnp.float32)], axis=1)
    upper_rows = jnp.where(col_ids[None, :] < PB, lead_cols, upper_rows)
    upper_rows, head_cols = (broadcast(upper_rows, "row", 0), broadcast(head_rows, "row", 0))
    product = jnp.dot(panel_rows, upper_rows, precision=precise)
    fill_cols = jnp.concatenate(
        [panel_rows, jnp.zeros((row_count, col_count - PB), jnp.float32)], axis=1
    )
    trailing = (row_ids[:, None] >= PB) & (col_ids[None, :] >= PB)
    updated = jnp.where(
        trailing, matrix - product, jnp.where(col_ids[None, :] < PB, fill_cols, 0.0)
    )
    head_top = jnp.concatenate(
        [head_cols, jnp.zeros((row_count - PB, target_width), jnp.float32)], axis=0
    )
    reduced = targets - jnp.dot(panel_rows, head_cols, precision=precise)
    reconstructor = jnp.where(row_ids[:, None] < PB, head_top, reduced)
    error_rows = target_width * lax.axis_size("col") // lax.axis_size("row")
    row_start = row_index * error_rows
    gathered = lax.all_gather(head_cols, "col", axis=1, tiled=True)
    head_needed = lax.dynamic_slice_in_dim(gathered, row_start, error_rows, 1)
    layer_all = jnp.repeat(tile_layer, TILE)
    col_start = col_index * target_width
    pos_rows = lax.dynamic_slice_in_dim(target_pos, row_start, error_rows, 1)
    pos_cols = lax.dynamic_slice_in_dim(target_pos, col_start, target_width, 1)
    layer_rows = lax.dynamic_slice_in_dim(layer_all, row_start, error_rows, 0)
    layer_cols = lax.dynamic_slice_in_dim(layer_all, col_start, target_width, 0)
    target_cov = target_covariance(
        pos_rows, pos_cols, layer_rows, layer_cols, layer_strength, layer_scale
    )
    error_cov = target_cov - lax.dot_general(
        head_needed,
        head_cols,
        (((0,), (0,)), ((), ())),
        precision=precise,
        preferred_element_type=jnp.float32,
    )
    return (updated, panel_rows, reconstructor, error_cov)


def solution(mesh):
    placed = (P("row", "col"), P("row"), P(), P("row", "col"), P(), P(), P(), P())
    return jax.shard_map(
        local,
        mesh=mesh,
        in_specs=placed,
        out_specs=(P("row", "col"), P("row", None), P("row", "col"), P("row", "col")),
        check_vma=False,
    )
```

profile of v0, /device:TPU:0, one launch (start us, length us, event | category | flops | bytes accessed | tf_op | source)
XLA Modules:
  0.0 518.4 jit_solution(5108484847680421361)
XLA Ops:
  7.2 6.1 %copy.26 = f32[768,1536]{0,1:T(8,128)} copy(f32[768,1536]{1,0:T(8,128)} %param.8) | data formatting | bytes 9437184 | tf_op args[0]
  13.3 0.4 convolution_reduce_fusion
  13.8 2.9 select_add_fusion
  16.6 2.2 copy-done.1
  18.8 0.7 slice_select_fusion
  19.7 144.5 %all-reduce.10.cloned.1.call-done = f32[256,256]{0,1:T(8,128)} async-done(((f32[256,256]{0,1:T(8,128)}), f32[256,256]{0,1:T(8,128)}) %all-reduce.10.cloned.1.call-update) | async-done | bytes 262160 | tf_op jit(solution)/shard_map/psum | solution.py:13
  164.2 1.1 copy.27
  165.2 1.0 fusion.11
  166.3 11.7 %cholesky.49 = f32[128,128]{1,0:T(8,128)S(1)} custom-call(f32[128,128]{1,0:T(8,128)S(1)} %cholesky.115), custom_call_target="Cholesky" | custom-call | tf_op jit(solution)/shard_map/jit(cholesky)/cholesky | solution.py:48
  178.0 0.1 copy.28
  178.1 9.8 %custom-call.21 = f32[1,128,128]{1,2,0:T(8,128)S(1)} custom-call(f32[1,128,128]{2,1,0:T(8,128)S(1)} %get-tuple-element.43), custom_call_target="InvertDiagBlocksLowerTriangular" | custom-call | tf_op jit(solution)/shard_map/jit(cholesky)/cholesky | solution.py:48
  187.9 0.2 fusion.17
  188.2 0.3 convolution_subtract_fusion.5
  188.5 11.7 %cholesky.103 = f32[128,128]{1,0:T(8,128)S(1)} custom-call(f32[128,128]{1,0:T(8,128)S(1)} %convolution_subtract_fusion.5), custom_call_target="Cholesky" | custom-call | tf_op jit(solution)/shard_map/jit(cholesky)/cholesky | solution.py:48
  200.4 0.6 compare_reduce_fusion
  202.5 4.4 while.1
  202.6 0.6 fusion.47
  203.2 1.4 dynamic-slice.11
  204.7 0.6 fusion.47
  205.3 1.4 dynamic-slice.11
  206.8 19.7 %custom-call.22 = f32[2,128,128]{1,2,0:T(8,128)S(1)} custom-call(f32[2,128,128]{2,1,0:T(8,128)S(1)} %get-tuple-element.11), custom_call_target="InvertDiagBlocksLowerTriangular" | custom-call | tf_op jit(solution)/shard_map/jit(_solve_triangular)/triangular_solve | solution.py:49
  226.5 2.0 fusion.5
  228.5 1.2 fusion.15
  229.8 1.2 convolution_subtract_fusion.4
  231.1 2.5 convolution_subtract_fusion
  233.6 0.9 fusion.21
  234.5 0.4 fusion.20
  234.9 0.7 maximum_select_fusion.1
  235.6 1.3 fusion.3
  237.1 1.2 slice_bitcast_fusion
  238.3 0.5 fusion.9
  238.9 0.5 convolution_subtract_fusion.2
  239.4 0.5 fusion.22
  239.9 1.0 fusion.8
  240.9 137.2 %all-reduce.14.cloned.1.call-done = (f32[256,1536]{1,0:T(8,128)}, f32[256,256]{0,1:T(8,128)}) async-done(((f32[256,1536]{1,0:T(8,128)}, f32[256,256]{0,1:T(8,128)}), (f32[256,1536]{1,0:T(8,128)}, f32[256,256]{0,1:T(8,128)})) %all-reduce.14.cloned.1.call-update) | async-done | bytes 1835024 | tf_op jit(solution)/shard_map/psum | solution.py:13
  378.1 0.3 copy.35
  378.7 0.7 constant_dynamic-slice_fusion.2
  379.4 0.8 constant_dynamic-slice_fusion.1
  380.3 0.1 multiply_add_fusion
  380.4 1.2 fusion.2
  381.6 76.2 %all-reduce.12.cloned.1.call-done = f32[768,256]{0,1:T(8,128)} async-done(((f32[768,256]{0,1:T(8,128)}), f32[768,256]{0,1:T(8,128)}) %all-reduce.12.cloned.1.call-update) | async-done | bytes 786448 | tf_op jit(solution)/shard_map/psum | solution.py:13
  457.8 2.3 copy.38
  460.1 9.2 %select_select_fusion = f32[768,1536]{0,1:T(8,128)} fusion(f32[768,256]{0,1:T(8,128)} %all-reduce.12.cloned.1.call-done, f32[768,1536]{0,1:T(8,128)} %copy-done.1, f32[256,1536]{1,0:T(8,128)S(1)} %copy-done.4, pred[1536]{0:T(1024)(128)(4,1)S(1)} %fusion.26, pred[768]{0:T(1024)(128)(4,1)S(1)} %fusion.29, pred[1536]{0:T(1024)(128)(4,1)S(1)} %fusion.27), kind=kOutput, calls=%fused_computation.2 | convolution fusion | flops 3628597248 | bytes 11800320 | tf_op jit(solution)/shard_map/dot_general | solution.py:58
  469.3 6.1 %copy.37 = f32[768,1536]{1,0:T(8,128)} copy(f32[768,1536]{0,1:T(8,128)} %select_select_fusion) | data formatting | bytes 9437184
  475.4 0.9 fusion.4
  476.3 1.1 copy.39
  477.5 32.4 %all-gather.2.cloned.1.call-done = f32[256,2048]{0,1:T(8,128)} async-done(((f32[256,256]{0,1:T(8,128)}), f32[256,2048]{0,1:T(8,128)}) %all-gather.2.cloned.1.call-update) | async-done | bytes 2097168 | tf_op jit(solution)/shard_map/all_gather | solution.py:73
  509.9 2.0 convolution_subtract_fusion.3
  (58 shorter events, 1.3 us)
Async XLA Ops:
  7.2 371.3 %copy-start = (s32[16]{0:T(128)S(1)}, s32[16]{0:T(128)}, u32[]{:S(2)}) copy-start(s32[16]{0:T(128)} %param.15) | copy-start | bytes 196
  7.2 157.0 %all-reduce.10.cloned.1.call-start = ((), (), s32[]{:S(2)}) async-start(), calls=%async_computation | async-start | bytes 524288 | tf_op jit(solution)/shard_map/psum | solution.py:13
  7.2 6.1 %copy-start.7 = (s32[768]{0:T(1024)S(1)}, s32[768]{0:T(1024)}, u32[]{:S(2)}) copy-start(s32[768]{0:T(1024)} %param.9) | copy-start | bytes 9220
  7.2 6.1 %copy-start.8 = (f32[6]{0:T(128)S(1)}, f32[6]{0:T(128)}, u32[]{:S(2)}) copy-start(f32[6]{0:T(128)} %param.10) | copy-start | bytes 76
  16.6 2.2 copy-start.1
  19.6 358.5 %all-reduce.14.cloned.1.call-start = ((), (), s32[]{:S(2)}) async-start(), calls=%async_computation.3 | async-start | bytes 3670016 | tf_op jit(solution)/shard_map/psum | solution.py:13
  237.0 141.2 %copy-start.5 = (f32[768,256]{1,0:T(8,128)S(1)}, f32[768,256]{1,0:T(8,128)}, u32[]{:S(2)}) copy-start(f32[768,256]{1,0:T(8,128)} %param.11) | copy-start | bytes 2359300
  237.0 141.4 %copy-start.9 = (f32[35]{0:T(128)S(1)}, f32[35]{0:T(128)}, u32[]{:S(2)}) copy-start(f32[35]{0:T(128)} %param.14) | copy-start | bytes 424
  237.0 220.8 %all-reduce.12.cloned.1.call-start = ((), (), s32[]{:S(2)}) async-start(), calls=%async_computation.1 | async-start | bytes 1572864 | tf_op jit(solution)/shard_map/psum | solution.py:13
  237.1 143.3 %copy-start.6 = (f32[35]{0:T(128)S(1)}, f32[35]{0:T(128)}, u32[]{:S(2)}) copy-start(f32[35]{0:T(128)} %param.13) | copy-start | bytes 424
  240.9 269.0 %all-gather.2.cloned.1.call-start = ((), (), s32[]{:S(2)}) async-start(), calls=%async_computation.2 | async-start | bytes 2359296 | tf_op jit(solution)/shard_map/all_gather | solution.py:73
  378.1 82.0 %copy-start.4 = (f32[256,1536]{1,0:T(8,128)S(1)}, f32[256,1536]{1,0:T(8,128)}, u32[]{:S(2)}) copy-start(f32[256,1536]{1,0:T(8,128)} %get-tuple-element.36) | copy-start | bytes 4718596
  469.3 6.1 %copy-start.2 = (f32[768,256]{0,1:T(8,128)S(1)}, f32[768,256]{0,1:T(8,128)}, u32[]{:S(2)}) copy-start(f32[768,256]{0,1:T(8,128)} %all-reduce.12.cloned.1.call-done) | copy-start | bytes 2359300
  469.3 6.1 %copy-start.3 = (f32[256,256]{0,1:T(8,128)S(1)}, f32[256,256]{0,1:T(8,128)}, u32[]{:S(2)}) copy-start(f32[256,256]{0,1:T(8,128)} %get-tuple-element.37) | copy-start | bytes 786436
Sparse Core Ops, SparseCore 0:
  19.7 144.4 all-reduce.9
  237.1 140.9 all-reduce.13
  381.3 76.4 all-reduce.11
  459.3 50.5 all-gather.1
where the time goes:
time: 519 us; the launch traced here: 518 us
  waiting for transfers between devices  390 us (75%)
  other arithmetic  62.7 us (12%)
  local copies, waits for them, and re-layouts  26.8 us (5%)
  matrix products  22.7 us (4%)
  between operations  15.5 us (3%)
    psum x3, waiting for transfers between devices, broadcast(): return lax.psum(jnp.where(mine, shard, jnp.zeros_like(shard)), axis)  358 us
    another operation x6, other arithmetic, local(): factor = jnp.linalg.cholesky(diag_block)  33.9 us
    all_gather x1, waiting for transfers between devices, local(): gathered = lax.all_gather(head_cols, 'col', axis=1, tiled=True)  32.4 us
    another operation x3, other arithmetic, local(): jax.scipy.linalg.solve_triangular(factor, matrix[:, :PB].T, lower=True)  19.7 us
    unnamed x25, local copies, waits for them, and re-layouts  18.1 us
  transfers between devices with their start and end apart: 4, of which 4 were waited for; matrix products, arithmetic and copies ran while one was open for 5% of the time, Pallas kernels for 0%

commit v1 on v0

--- a/solution.py
+++ b/solution.py
@@ -70,7 +70,10 @@
     reconstructor = jnp.where(row_ids[:, None] < PB, head_top, reduced)
     error_rows = target_width * lax.axis_size("col") // lax.axis_size("row")
     row_start = row_index * error_rows
-    gathered = lax.all_gather(head_cols, "col", axis=1, tiled=True)
+    size = lax.axis_size("col")
+    pieces = jnp.stack([head_cols for _ in range(size)])
+    pieces = lax.all_to_all(pieces, "col", split_axis=0, concat_axis=0)
+    gathered = jnp.concatenate(pieces, axis=1)
     head_needed = lax.dynamic_slice_in_dim(gathered, row_start, error_rows, 1)
     layer_all = jnp.repeat(tile_layer, TILE)
     col_start = col_index * target_width

time: 519 us -> 499 us (0.961)
  waiting for transfers between devices: 390 us -> 365 us
    all_gather x1 -> x0, waiting for transfers between devices: 32.4 us -> none  [local(): gathered = lax.all_gather(head_cols, 'col', axis=1, tiled=True)]
    psum x3, waiting for transfers between devices: 358 us -> 365 us  [broadcast(): return lax.psum(jnp.where(mine, shard, jnp.zeros_like(shard)), axis)]
  transfers between devices with their start and end apart: 4 -> 4, of which waited for: 4 -> 3; matrix products, arithmetic and copies ran while one was open for 5% -> 6% of each run, Pallas kernels for 0% -> 0%
where the time goes in v1:
time: 499 us; the launch traced here: 498 us
  waiting for transfers between devices  365 us (73%)
  other arithmetic  62.7 us (13%)
  local copies, waits for them, and re-layouts  29.4 us (6%)
  matrix products  20.9 us (4%)
  between operations  15.4 us (3%)
    psum x3, waiting for transfers between devices, broadcast(): return lax.psum(jnp.where(mine, shard, jnp.zeros_like(shard)), axis)  365 us
    another operation x6, other arithmetic, local(): factor = jnp.linalg.cholesky(diag_block)  33.9 us
    another operation x3, other arithmetic, local(): jax.scipy.linalg.solve_triangular(factor, matrix[:, :PB].T, lower=True)  19.7 us
    unnamed x25, local copies, waits for them, and re-layouts  18.1 us
  transfers between devices with their start and end apart: 4, of which 3 were waited for; matrix products, arithmetic and copies ran while one was open for 6% of the time, Pallas kernels for 0%

profile of v1, /device:TPU:0, one launch (start us, length us, event | category | flops | bytes accessed | tf_op | source)
XLA Modules:
  0.0 498.2 jit_solution(16146570833556749602)
XLA Ops:
  7.2 6.1 %copy.41 = f32[768,1536]{0,1:T(8,128)} copy(f32[768,1536]{1,0:T(8,128)} %param.8) | data formatting | bytes 9437184 | tf_op args[0]
  13.3 0.4 convolution_reduce_fusion
  13.8 2.9 select_add_fusion
  16.6 2.2 copy-done.1
  18.8 0.7 slice_select_fusion
  19.6 0.7 constant_dynamic-slice_fusion.2
  20.4 143.7 %all-reduce.10.cloned.1.call-done = f32[256,256]{0,1:T(8,128)} async-done(((f32[256,256]{0,1:T(8,128)}), f32[256,256]{0,1:T(8,128)}) %all-reduce.10.cloned.1.call-update) | async-done | bytes 262160 | tf_op jit(solution)/shard_map/psum | solution.py:13
  164.2 1.1 copy.42
  165.2 1.0 fusion.11
  166.3 11.7 %cholesky.49 = f32[128,128]{1,0:T(8,128)S(1)} custom-call(f32[128,128]{1,0:T(8,128)S(1)} %cholesky.115), custom_call_target="Cholesky" | custom-call | tf_op jit(solution)/shard_map/jit(cholesky)/cholesky | solution.py:48
  178.1 9.8 %custom-call.21 = f32[1,128,128]{1,2,0:T(8,128)S(1)} custom-call(f32[1,128,128]{2,1,0:T(8,128)S(1)} %get-tuple-element.51), custom_call_target="InvertDiagBlocksLowerTriangular" | custom-call | tf_op jit(solution)/shard_map/jit(cholesky)/cholesky | solution.py:48
  187.9 0.2 fusion.17
  188.2 0.3 convolution_subtract_fusion.5
  188.5 11.7 %cholesky.103 = f32[128,128]{1,0:T(8,128)S(1)} custom-call(f32[128,128]{1,0:T(8,128)S(1)} %convolution_subtract_fusion.5), custom_call_target="Cholesky" | custom-call | tf_op jit(solution)/shard_map/jit(cholesky)/cholesky | solution.py:48
  200.4 0.6 compare_reduce_fusion
  202.5 4.4 while.1
  202.6 0.6 fusion.47
  203.2 1.4 dynamic-slice.11
  204.7 0.6 fusion.47
  205.3 1.4 dynamic-slice.11
  206.8 19.7 %custom-call.22 = f32[2,128,128]{1,2,0:T(8,128)S(1)} custom-call(f32[2,128,128]{2,1,0:T(8,128)S(1)} %get-tuple-element.11), custom_call_target="InvertDiagBlocksLowerTriangular" | custom-call | tf_op jit(solution)/shard_map/jit(_solve_triangular)/triangular_solve | solution.py:49
  226.5 2.0 fusion.5
  228.5 0.3 fusion.15
  228.8 0.3 convolution_subtract_fusion.4
  229.3 2.5 convolution_subtract_fusion
  231.8 0.9 fusion.21
  232.7 0.4 fusion.20
  233.1 0.7 maximum_select_fusion.1
  233.8 1.3 fusion.3
  235.3 0.3 copy.51
  235.7 0.8 constant_dynamic-slice_fusion.1
  236.6 0.1 multiply_add_fusion
  236.7 1.2 slice_bitcast_fusion
  237.9 0.5 fusion.9
  238.5 0.5 convolution_subtract_fusion.2
  239.0 0.5 fusion.22
  239.5 1.0 fusion.8
  240.5 135.7 %all-reduce.14.cloned.1.call-done = (f32[256,1536]{1,0:T(8,128)}, f32[256,256]{0,1:T(8,128)}) async-done(((f32[256,1536]{1,0:T(8,128)}, f32[256,256]{0,1:T(8,128)}), (f32[256,1536]{1,0:T(8,128)}, f32[256,256]{0,1:T(8,128)})) %all-reduce.14.cloned.1.call-update) | async-done | bytes 1835024 | tf_op jit(solution)/shard_map/psum | solution.py:13
  376.2 2.6 stack.2
  378.9 4.6 all-to-all-start
  383.5 1.2 fusion.2
  384.7 85.4 %all-reduce.12.cloned.1.call-done = f32[768,256]{0,1:T(8,128)} async-done(((f32[768,256]{0,1:T(8,128)}), f32[768,256]{0,1:T(8,128)}) %all-reduce.12.cloned.1.call-update) | async-done | bytes 786448 | tf_op jit(solution)/shard_map/psum | solution.py:13
  470.0 2.3 copy.54
  472.3 9.2 %select_select_fusion = f32[768,1536]{0,1:T(8,128)} fusion(f32[768,256]{0,1:T(8,128)} %all-reduce.12.cloned.1.call-done, f32[768,1536]{0,1:T(8,128)} %copy-done.1, f32[256,1536]{1,0:T(8,128)S(1)} %copy-done.4, pred[1536]{0:T(1024)(128)(4,1)S(1)} %fusion.26, pred[768]{0:T(1024)(128)(4,1)S(1)} %fusion.29, pred[1536]{0:T(1024)(128)(4,1)S(1)} %fusion.27), kind=kOutput, calls=%fused_computation.2 | convolution fusion | flops 3628597248 | bytes 11800320 | tf_op jit(solution)/shard_map/dot_general | solution.py:58
  481.5 6.1 %copy.53 = f32[768,1536]{1,0:T(8,128)} copy(f32[768,1536]{0,1:T(8,128)} %select_select_fusion) | data formatting | bytes 9437184
  487.6 0.9 fusion.4
  488.5 1.1 copy.55
  489.7 2.0 convolution_subtract_fusion.3
  (58 shorter events, 1.4 us)
Async XLA Ops:
  7.2 13.2 %copy-start = (s32[16]{0:T(128)S(1)}, s32[16]{0:T(128)}, u32[]{:S(2)}) copy-start(s32[16]{0:T(128)} %param.15) | copy-start | bytes 196
  7.2 157.0 %all-reduce.10.cloned.1.call-start = ((), (), s32[]{:S(2)}) async-start(), calls=%async_computation.1 | async-start | bytes 524288 | tf_op jit(solution)/shard_map/psum | solution.py:13
  7.2 6.1 %copy-start.7 = (s32[768]{0:T(1024)S(1)}, s32[768]{0:T(1024)}, u32[]{:S(2)}) copy-start(s32[768]{0:T(1024)} %param.9) | copy-start | bytes 9220
  7.2 6.1 %copy-start.8 = (f32[6]{0:T(128)S(1)}, f32[6]{0:T(128)}, u32[]{:S(2)}) copy-start(f32[6]{0:T(128)} %param.10) | copy-start | bytes 76
  16.6 2.2 copy-start.1
  18.8 209.7 %copy-start.5 = (f32[768,256]{1,0:T(8,128)S(1)}, f32[768,256]{1,0:T(8,128)}, u32[]{:S(2)}) copy-start(f32[768,256]{1,0:T(8,128)} %param.11) | copy-start | bytes 2359300
  19.6 356.7 %all-reduce.14.cloned.1.call-start = ((), (), s32[]{:S(2)}) async-start(), calls=%async_computation.3 | async-start | bytes 3670016 | tf_op jit(solution)/shard_map/psum | solution.py:13
  231.8 3.7 copy-start.9
  235.2 234.8 %all-reduce.12.cloned.1.call-start = ((), (), s32[]{:S(2)}) async-start(), calls=%async_computation.2 | async-start | bytes 1572864 | tf_op jit(solution)/shard_map/psum | solution.py:13
  239.5 143.9 %copy-start.6 = (f32[35]{0:T(128)S(1)}, f32[35]{0:T(128)}, u32[]{:S(2)}) copy-start(f32[35]{0:T(128)} %param.13) | copy-start | bytes 424
  376.2 96.1 %copy-start.4 = (f32[256,1536]{1,0:T(8,128)S(1)}, f32[256,1536]{1,0:T(8,128)}, u32[]{:S(2)}) copy-start(f32[256,1536]{1,0:T(8,128)} %get-tuple-element.44) | copy-start | bytes 4718596
  378.9 110.8 %all-to-all-start = ((f32[8,256,256]{1,2,0:T(8,128)}), f32[8,256,256]{1,2,0:T(8,128)}, u32[]{:S(2)}, u32[]{:S(2)}) async-start(f32[8,256,256]{1,2,0:T(8,128)} %stack.2), calls=%async_computation | async-start | bytes 4194304 | tf_op jit(solution)/shard_map/all_to_all | solution.py:75
  481.5 6.1 %copy-start.2 = (f32[768,256]{0,1:T(8,128)S(1)}, f32[768,256]{0,1:T(8,128)}, u32[]{:S(2)}) copy-start(f32[768,256]{0,1:T(8,128)} %all-reduce.12.cloned.1.call-done) | copy-start | bytes 2359300
  481.5 6.1 %copy-start.3 = (f32[256,256]{0,1:T(8,128)S(1)}, f32[256,256]{0,1:T(8,128)}, u32[]{:S(2)}) copy-start(f32[256,256]{0,1:T(8,128)} %get-tuple-element.45) | copy-start | bytes 786436
Sparse Core Ops, SparseCore 0:
  19.7 144.4 all-reduce.9
  235.3 140.8 all-reduce.13
  379.5 90.5 all-reduce.11
